TPU v7x, 32 devices: a whole 2x2x4 slice. The times are simulated.
32 devices in a mesh: grp: 2 (over core), ep: 16 (over z, y, x).
Axes of the slice: x: 2, y: 2, z: 4, core: 2. Of those that a mesh axis runs over, the one named last changes fastest.
Arguments:
- out_grad: bfloat16 [16384, 2048], P(('grp', 'ep')), may hold values from -0.5 to 0.5
- probs: float32 [16384, 8], P(('grp', 'ep')), may hold values from 0.02 to 0.5
- dest: int32 [16384, 8], P(('grp', 'ep')), may hold values from -1 to 49151, as said below
- replica_owner: int32 [2, 16], P('grp'), may hold values from 0 to 15, as said below
- gate_up: bfloat16 [98304, 1536], P(('grp', 'ep')), may hold values from -6 to 6
Outputs:
- d_down: float32 [16, 768, 2048], P('ep', None, 'grp')
Inputs may be any that keep to these rules, and one draw needn't show every extreme that they name: `dest`: copies of one token name distinct rows; a device's copies to slot buffer (j, s) fill the rows of that buffer's block for the device, which is the device's ep index times 96 onward, from its start without gaps; in every draw some device fills its block of some buffer, all 96 rows, and copies beyond a block are dropped. `replica_owner`: each entry names an expert that has its primary slot on that ep index of the group.
All inputs are finite; a program needn't handle non-finite values.
Results may differ from a plain program's by a relative error of at most 0.005.
Values may be sent and summed in bfloat16 or wider, within the bound.
A program may use at most 128 MiB of HBM per device.

v0:
```python
import jax
import jax.numpy as jnp
from jax import lax
from jax.sharding import PartitionSpec as P


def on_device(out_grad, probs, dest, replica_owner, gate_up):
    n_ep = lax.axis_size("ep")
    tokens = out_grad.shape[0]
    width = out_grad.shape[1]
    top = probs.shape[1]
    cap = gate_up.shape[0] // 2
    hidden = gate_up.shape[1] // 2
    per_src = cap // n_ep
    flat = dest.reshape(-1)
    device_of = flat // (2 * cap)
    within = flat % (2 * cap)
    slot_lookup = within // cap
    place = within % per_src
    target = device_of * 2 * per_src + slot_lookup * per_src + place
    target = jnp.where(flat >= 0, target, 2 * cap)
    copy_of = (
        jnp.full((2 * cap,), -1, jnp.int32)
        .at[target]
        .set(jnp.arange(tokens * top, dtype=jnp.int32), mode="drop")
    )
    safe = jnp.maximum(copy_of, 0)
    weight = jnp.where(copy_of >= 0, probs.reshape(-1)[safe], 0.0)
    outgoing = (weight[:, None] * out_grad[safe // top].astype(jnp.float32)).astype(jnp.bfloat16)
    outgoing = outgoing.reshape(n_ep, 2, per_src, width)
    incoming = lax.all_to_all(outgoing, "ep", split_axis=0, concat_axis=2, tiled=True)
    grads = incoming.reshape(2, cap, width)
    act = jax.nn.silu(gate_up[:, :hidden].astype(jnp.float32)) * gate_up[:, hidden:].astype(
        jnp.float32
    )
    act = act.astype(jnp.bfloat16).reshape(2, cap, hidden)
    tiles = jnp.einsum("sch,scd->shd", act, grads, preferred_element_type=jnp.float32).astype(
        jnp.bfloat16
    )
    owners = replica_owner[0]
    experts = jnp.arange(n_ep, dtype=jnp.int32)
    received = lax.all_to_all(tiles[1], "ep", split_axis=0, concat_axis=0, tiled=True)
    pieces = received.reshape(n_ep, -1)
    primary = tiles[0].astype(jnp.float32)
    select = (owners[None, :] == experts[:, None]).astype(jnp.bfloat16)
    block_sums = jnp.dot(select, pieces, preferred_element_type=jnp.float32).reshape(-1, width)
    owned = lax.all_to_all(block_sums, "ep", split_axis=0, concat_axis=0, tiled=True)
    owned = owned + primary
    result = lax.psum_scatter(owned, "grp", scatter_dimension=1, tiled=True)
    return result[None]


def solution(mesh):
    in_specs = (
        P(("grp", "ep"), None),
        P(("grp", "ep"), None),
        P(("grp", "ep"), None),
        P("grp", None),
        P(("grp", "ep"), None),
    )
    out_specs = P("ep", None, "grp")
    return jax.shard_map(
        on_device, mesh=mesh, in_specs=in_specs, out_specs=out_specs, check_vma=False
    )
```

profile of v0, /device:TPU:0, one launch (start us, length us, event | category | flops | bytes accessed | tf_op | source)
XLA Modules:
  0.0 633.6 jit_solution(17132969857570626571)
XLA Ops:
  6.5 0.9 broadcast_divide_fusion
  7.4 0.7 sign_compare_fusion
  8.3 0.2 div.41
  8.6 0.2 rem.59
  8.9 0.2 ge.17
  9.3 0.2 ne.104
  9.5 0.2 compare_select_fusion
  9.7 15.5 %scatter_custom_fusion = s32[3072]{0:T(1024)S(1)} fusion(s32[4096]{0:T(1024)S(1)} %bitcast.41, s32[4096]{0:T(1024)S(1)} %iota.7, s32[]{:T(128)} %constant.55.clone.1), kind=kCustom, calls=%fused_computation.39 | custom fusion | bytes 12292 | tf_op jit(solution)/shard_map/scatter | solution.py:25
  25.3 0.8 copy.23
  26.3 17.4 %gather_fusion = f32[3072]{0:T(1024)S(1)} fusion(f32[4096]{0:T(1024)S(1)} %reshape.175, s32[3072]{0:T(1024)S(1)} %get-tuple-element.9), kind=kCustom, calls=%fused_computation | custom fusion | bytes 36864 | tf_op jit(solution)/shard_map/gather | solution.py:28
  43.8 16.0 %gather_fusion.1 = bf16[3072,2048]{1,0:T(8,128)(2,1)} fusion(bf16[512,2048]{1,0:T(8,128)(2,1)S(1)} %copy-done, s32[3072]{0:T(1024)S(1)} %get-tuple-element.10), kind=kCustom, calls=%fused_computation.1 | custom fusion | bytes 25178112 | tf_op jit(solution)/shard_map/gather | solution.py:29
  59.8 11.1 %fusion = bf16[16,2,96,2048]{3,2,1,0:T(8,128)(2,1)} fusion(bf16[16,2,96,2048]{3,2,1,0:T(8,128)(2,1)} %bitcast.34, f32[16,2,96]{2,1,0:T(2,128)S(1)} %mul.47), kind=kLoop, calls=%fused_computation.4 | loop fusion | flops 18874368 | bytes 25178112 | tf_op jit(solution)/shard_map/convert_element_type | solution.py:29
  70.9 8.4 %all-to-all-start = ((bf16[16,2,96,2048]{3,2,1,0:T(8,128)(2,1)}), bf16[16,2,96,2048]{3,2,1,0:T(8,128)(2,1)}, u32[]{:S(2)}, u32[]{:S(2)}) async-start(bf16[16,2,96,2048]{3,2,1,0:T(8,128)(2,1)} %fusion), calls=%async_computation | async-start | bytes 25165824 | tf_op jit(solution)/shard_map/all_to_all | solution.py:31
  79.4 8.0 %fusion.5 = bf16[3072,768]{1,0:T(8,128)(2,1)} fusion(bf16[3072,1536]{1,0:T(8,128)(2,1)} %param.9), kind=kLoop, calls=%fused_computation.11 | loop fusion | flops 18874368 | bytes 14155776 | tf_op jit(solution)/shard_map/convert_element_type | solution.py:36
  87.4 229.1 %all-to-all-done = bf16[16,2,96,2048]{3,2,1,0:T(8,128)(2,1)} async-done(((bf16[16,2,96,2048]{3,2,1,0:T(8,128)(2,1)}), bf16[16,2,96,2048]{3,2,1,0:T(8,128)(2,1)}, u32[]{:S(2)}, u32[]{:S(2)}) %all-to-all-start) | async-done | bytes 12582944 | tf_op jit(solution)/shard_map/all_to_all | solution.py:31
  316.5 6.5 %copy.24 = bf16[1,2,16,96,2048]{4,3,2,1,0:T(8,128)(2,1)S(1)} copy(bf16[1,2,16,96,2048]{4,3,1,2,0:T(8,128)(2,1)} %bitcast.6) | data formatting | bytes 25165824 | tf_op jit(solution)/shard_map/all_to_all | solution.py:31
  323.0 12.0 %convolution_convert_fusion = bf16[2,768,2048]{2,1,0:T(8,128)(2,1)} fusion(bf16[2,1536,768]{2,1,0:T(8,128)(2,1)S(1)} %bitcast.40, bf16[2,1536,2048]{2,1,0:T(8,128)(2,1)S(1)} %bitcast.35), kind=kOutput, calls=%fused_computation.13 | convolution fusion | flops 9666822144 | bytes 23592960 | tf_op jit(solution)/shard_map/sch,scd->shd/dot_general | solution.py:37
  335.0 1.9 slice-done.2
  336.9 124.8 %all_to_all.33 = bf16[16,48,2048]{2,1,0:T(8,128)(2,1)S(1)} all-to-all(bf16[16,48,2048]{2,1,0:T(8,128)(2,1)S(1)} %bitcast.38), channel_id=1, replica_groups=mesh['grp'=2,'ep'=16] {'ep'}, dimensions={0} | all-to-all | bytes 6291456 | tf_op jit(solution)/shard_map/all_to_all | solution.py:42
  461.7 3.6 fusion.6
  465.3 3.6 copy.27
  468.9 141.8 %all_to_all.34 = f32[16,48,2048]{2,1,0:T(8,128)S(1)} all-to-all(f32[16,48,2048]{2,1,0:T(8,128)S(1)} %copy.27), channel_id=1, replica_groups=mesh['grp'=2,'ep'=16] {'ep'}, dimensions={0} | all-to-all | bytes 12582912 | tf_op jit(solution)/shard_map/all_to_all | solution.py:47
  610.8 3.7 convert_add_fusion
  614.5 12.3 %reduce-scatter.2.cloned.1.call-done = f32[768,1024]{1,0:T(8,128)} async-done(((f32[768,2048]{1,0:T(8,128)}), f32[768,1024]{1,0:T(8,128)}) %reduce-scatter.2.cloned.1.call-update) | async-done | bytes 3145744 | tf_op jit(solution)/shard_map/reduce_scatter | solution.py:49
  (25 shorter events, 0.9 us)
Async XLA Ops:
  6.5 37.3 %copy-start = (bf16[512,2048]{1,0:T(8,128)(2,1)S(1)}, bf16[512,2048]{1,0:T(8,128)(2,1)}, u32[]{:S(2)}) copy-start(bf16[512,2048]{1,0:T(8,128)(2,1)} %param.5) | copy-start | bytes 6291460
  70.9 245.6 %all-to-all-start = ((bf16[16,2,96,2048]{3,2,1,0:T(8,128)(2,1)}), bf16[16,2,96,2048]{3,2,1,0:T(8,128)(2,1)}, u32[]{:S(2)}, u32[]{:S(2)}) async-start(bf16[16,2,96,2048]{3,2,1,0:T(8,128)(2,1)} %fusion), calls=%async_computation | async-start | bytes 25165824 | tf_op jit(solution)/shard_map/all_to_all | solution.py:31
  79.3 547.4 %reduce-scatter.2.cloned.1.call-start = ((), (), s32[]{:S(2)}) async-start(), calls=%async_computation.4 | async-start | bytes 9437184 | tf_op jit(solution)/shard_map/reduce_scatter | solution.py:49
  316.5 6.5 %copy-start.2 = (bf16[3072,768]{1,0:T(8,128)(2,1)S(1)}, bf16[3072,768]{1,0:T(8,128)(2,1)}, u32[]{:S(2)}) copy-start(bf16[3072,768]{1,0:T(8,128)(2,1)} %fusion.5) | copy-start | bytes 14155780
  335.0 1.9 slice-start.2
  335.0 126.7 %copy-start.3 = (s32[1,16]{1,0:T(1,128)S(1)}, s32[1,16]{1,0:T(1,128)}, u32[]{:S(2)}) copy-start(s32[1,16]{1,0:T(1,128)} %param.8) | copy-start | bytes 196
  465.3 145.5 %slice-start = ((s8[6291456]{0:T(1024)(128)(4,1)}), s8[4194304]{0:T(1024)(128)(4,1)S(1)}, s32[]{:S(2)}) async-start(s8[6291456]{0:T(1024)(128)(4,1)} %bitcast.36), calls=%async_computation.5 | async-start | bytes 8388608
  468.9 141.8 %slice-start.1 = ((s8[6291456]{0:T(1024)(128)(4,1)}), s8[2097152]{0:T(1024)(128)(4,1)S(1)}, s32[]{:S(2)}) async-start(s8[6291456]{0:T(1024)(128)(4,1)} %bitcast.36), calls=%async_computation.6 | async-start | bytes 4194304
  610.7 16.0 %copy-start.1 = (bf16[512,2048]{1,0:T(8,128)(2,1)S(1)}, bf16[512,2048]{1,0:T(8,128)(2,1)}, u32[]{:S(2)}) copy-start(bf16[512,2048]{1,0:T(8,128)(2,1)} %param.5) | copy-start | bytes 6291460
Sparse Core Ops, SparseCore 0:
  614.6 12.1 reduce-scatter.1
where the time goes:
time: 634 us
  blocking collectives  267 us (42%)
  waiting for transfers between devices  241 us (38%)
  local copies, waits for them, and re-layouts  63.3 us (10%)
  other arithmetic  24.7 us (4%)
  matrix products  15.6 us (2%)
  between operations  13.6 us (2%)
  starting transfers between devices  8.43 us (1%)
    all_to_all x1, waiting for transfers between devices, on_device(): lax.all_to_all(outgoing, 'ep', split_axis=0, concat_axis=2, tiled=True)  229 us
    all_to_all x1, blocking collectives, on_device(): lax.all_to_all(block_sums, 'ep', split_axis=0, concat_axis=0, tiled=True)  142 us
    all_to_all x1, blocking collectives, on_device(): lax.all_to_all(tiles[1], 'ep', split_axis=0, concat_axis=0, tiled=True)  125 us
    gather x1, local copies, waits for them, and re-layouts, on_device(): weight = jnp.where(copy_of >= 0, probs.reshape(-1)[safe], 0.0)  17.4 us
    gather x1, local copies, waits for them, and re-layouts, on_device(): out_grad[safe // top].astype(jnp.float32)  16 us
    scatter x1, local copies, waits for them, and re-layouts, on_device(): copy_of = jnp.full((2 * cap,), -1, jnp.int32).at[target].set(jnp.arange(t...  15.5 us
  transfers between devices with their start and end apart: 2, of which 2 were waited for; matrix products, arithmetic and copies ran while one was open for 1% of the time, Pallas kernels for 0%

commit v1 on v0

--- a/solution.py
+++ b/solution.py
@@ -28,7 +28,10 @@
     weight = jnp.where(copy_of >= 0, probs.reshape(-1)[safe], 0.0)
     outgoing = (weight[:, None] * out_grad[safe // top].astype(jnp.float32)).astype(jnp.bfloat16)
     outgoing = outgoing.reshape(n_ep, 2, per_src, width)
-    incoming = lax.all_to_all(outgoing, "ep", split_axis=0, concat_axis=2, tiled=True)
+    incoming = jnp.concatenate(
+        lax.all_to_all(jnp.stack(jnp.split(outgoing, lax.axis_size("ep"), axis=0)), "ep", 0, 0),
+        axis=2,
+    )
     grads = incoming.reshape(2, cap, width)
     act = jax.nn.silu(gate_up[:, :hidden].astype(jnp.float32)) * gate_up[:, hidden:].astype(
         jnp.float32

time: 634 us -> 649 us (1.024)
  local copies, waits for them, and re-layouts: 63.3 us -> 81.5 us
    unnamed x13 -> x28, local copies, waits for them, and re-layouts: 0.86 us -> 15.5 us
where the time goes in v1:
time: 649 us; the launch traced here: 648 us
  blocking collectives  267 us (41%)
  waiting for transfers between devices  241 us (37%)
  local copies, waits for them, and re-layouts  81.5 us (13%)
  other arithmetic  20.8 us (3%)
  matrix products  15.6 us (2%)
  between operations  13.6 us (2%)
  starting transfers between devices  8.43 us (1%)
    all_to_all x1, waiting for transfers between devices, on_device(): lax.all_to_all(jnp.stack(jnp.split(outgoing, lax.axis_size('ep'), axis=0)...  229 us
    all_to_all x1, blocking collectives, on_device(): lax.all_to_all(block_sums, 'ep', split_axis=0, concat_axis=0, tiled=True)  142 us
    all_to_all x1, blocking collectives, on_device(): lax.all_to_all(tiles[1], 'ep', split_axis=0, concat_axis=0, tiled=True)  125 us
    gather x1, local copies, waits for them, and re-layouts, on_device(): weight = jnp.where(copy_of >= 0, probs.reshape(-1)[safe], 0.0)  17.4 us
    gather x1, local copies, waits for them, and re-layouts, on_device(): out_grad[safe // top].astype(jnp.float32)  16 us
    scatter x1, local copies, waits for them, and re-layouts, on_device(): copy_of = jnp.full((2 * cap,), -1, jnp.int32).at[target].set(jnp.arange(t...  15.5 us
    unnamed x28, local copies, waits for them, and re-layouts  15.5 us
  transfers between devices with their start and end apart: 2, of which 2 were waited for; matrix products, arithmetic and copies ran while one was open for 1% of the time, Pallas kernels for 0%

profile of v1, /device:TPU:0, one launch (start us, length us, event | category | flops | bytes accessed | tf_op | source)
XLA Modules:
  0.0 648.1 jit_solution(3947122857836698353)
XLA Ops:
  9.7 15.5 %scatter_custom_fusion = s32[3072]{0:T(1024)S(1)} fusion(s32[4096]{0:T(1024)S(1)} %bitcast.68, s32[4096]{0:T(1024)S(1)} %iota.7, s32[]{:T(128)} %constant.55.clone.1), kind=kCustom, calls=%fused_computation.54 | custom fusion | bytes 12292 | tf_op jit(solution)/shard_map/scatter | solution.py:25
  26.3 17.4 %gather_fusion = f32[3072]{0:T(1024)S(1)} fusion(f32[4096]{0:T(1024)S(1)} %reshape.198, s32[3072]{0:T(1024)S(1)} %get-tuple-element.25), kind=kCustom, calls=%fused_computation | custom fusion | bytes 36864 | tf_op jit(solution)/shard_map/gather | solution.py:28
  43.7 16.0 %gather_fusion.1 = bf16[3072,2048]{1,0:T(8,128)(2,1)} fusion(bf16[512,2048]{1,0:T(8,128)(2,1)S(1)} %copy-done, s32[3072]{0:T(1024)S(1)} %get-tuple-element.26), kind=kCustom, calls=%fused_computation.1 | custom fusion | bytes 25178112 | tf_op jit(solution)/shard_map/gather | solution.py:29
  59.7 7.2 %multiply_convert_fusion = bf16[3072,2048]{1,0:T(8,128)(2,1)S(1)} fusion(bf16[3072,2048]{1,0:T(8,128)(2,1)} %gather_fusion.1, f32[3072]{0:T(1024)S(1)} %compare_select_fusion.2), kind=kLoop, calls=%fused_computation.3 | loop fusion | flops 18874368 | bytes 25178112 | tf_op jit(solution)/shard_map/convert_element_type | solution.py:29
  66.9 2.2 fusion.17
  69.2 1.0 constant_dynamic-update-slice_fusion.15
  72.2 1.0 constant_dynamic-update-slice_fusion.12
  73.1 1.0 constant_dynamic-update-slice_fusion.11
  75.1 1.0 constant_dynamic-update-slice_fusion.9
  78.0 1.0 constant_dynamic-update-slice_fusion.6
  80.9 1.0 constant_dynamic-update-slice_fusion.3
  83.9 1.0 constant_dynamic-update-slice_fusion
  84.9 8.4 %all-to-all-start = ((bf16[16,1,2,96,2048]{4,3,2,1,0:T(8,128)(2,1)}), bf16[16,1,2,96,2048]{4,3,2,1,0:T(8,128)(2,1)}, u32[]{:S(2)}, u32[]{:S(2)}) async-start(bf16[16,1,2,96,2048]{4,3,2,1,0:T(8,128)(2,1)} %constant_dynamic-update-slice_fusion), calls=%async_computation | async-start | bytes 25165824 | tf_op jit(solution)/shard_map/all_to_all | solution.py:32
  93.3 8.0 %fusion.4 = bf16[3072,768]{1,0:T(8,128)(2,1)} fusion(bf16[3072,1536]{1,0:T(8,128)(2,1)} %param.9), kind=kLoop, calls=%fused_computation.10 | loop fusion | flops 18874368 | bytes 14155776 | tf_op jit(solution)/shard_map/convert_element_type | solution.py:39
  101.3 229.1 %all-to-all-done = bf16[16,1,2,96,2048]{4,3,2,1,0:T(8,128)(2,1)} async-done(((bf16[16,1,2,96,2048]{4,3,2,1,0:T(8,128)(2,1)}), bf16[16,1,2,96,2048]{4,3,2,1,0:T(8,128)(2,1)}, u32[]{:S(2)}, u32[]{:S(2)}) %all-to-all-start) | async-done | bytes 12582944 | tf_op jit(solution)/shard_map/all_to_all | solution.py:32
  330.5 6.5 copy.53
  337.0 12.0 %convolution_convert_fusion = bf16[2,768,2048]{2,1,0:T(8,128)(2,1)} fusion(bf16[2,1536,768]{2,1,0:T(8,128)(2,1)S(1)} %bitcast.51, bf16[2,1536,2048]{2,1,0:T(8,128)(2,1)S(1)} %bitcast.46), kind=kOutput, calls=%fused_computation.12 | convolution fusion | flops 9666822144 | bytes 23592960 | tf_op jit(solution)/shard_map/sch,scd->shd/dot_general | solution.py:40
  348.9 2.3 slice.36
  351.3 124.8 %all_to_all.23 = bf16[16,48,2048]{2,1,0:T(8,128)(2,1)S(1)} all-to-all(bf16[16,48,2048]{2,1,0:T(8,128)(2,1)S(1)} %bitcast.47), channel_id=1, replica_groups=mesh['grp'=2,'ep'=16] {'ep'}, dimensions={0} | all-to-all | bytes 6291456 | tf_op jit(solution)/shard_map/all_to_all | solution.py:45
  476.1 3.6 fusion.5
  479.6 3.6 copy.56
  483.3 141.9 %all_to_all.24 = f32[16,48,2048]{2,1,0:T(8,128)S(1)} all-to-all(f32[16,48,2048]{2,1,0:T(8,128)S(1)} %copy.56), channel_id=1, replica_groups=mesh['grp'=2,'ep'=16] {'ep'}, dimensions={0} | all-to-all | bytes 12582912 | tf_op jit(solution)/shard_map/all_to_all | solution.py:50
  625.2 3.7 convert_add_fusion
  629.0 12.3 %reduce-scatter.2.cloned.1.call-done = f32[768,1024]{1,0:T(8,128)} async-done(((f32[768,2048]{1,0:T(8,128)}), f32[768,1024]{1,0:T(8,128)}) %reduce-scatter.2.cloned.1.call-update) | async-done | bytes 3145744 | tf_op jit(solution)/shard_map/reduce_scatter | solution.py:52
  (40 shorter events, 12.9 us)
Async XLA Ops:
  6.5 37.2 %copy-start = (bf16[512,2048]{1,0:T(8,128)(2,1)S(1)}, bf16[512,2048]{1,0:T(8,128)(2,1)}, u32[]{:S(2)}) copy-start(bf16[512,2048]{1,0:T(8,128)(2,1)} %param.5) | copy-start | bytes 6291460
  84.9 245.6 %all-to-all-start = ((bf16[16,1,2,96,2048]{4,3,2,1,0:T(8,128)(2,1)}), bf16[16,1,2,96,2048]{4,3,2,1,0:T(8,128)(2,1)}, u32[]{:S(2)}, u32[]{:S(2)}) async-start(bf16[16,1,2,96,2048]{4,3,2,1,0:T(8,128)(2,1)} %constant_dynamic-update-slice_fusion), calls=%async_computation | async-start | bytes 25165824 | tf_op jit(solution)/shard_map/all_to_all | solution.py:32
  93.3 548.0 %reduce-scatter.2.cloned.1.call-start = ((), (), s32[]{:S(2)}) async-start(), calls=%async_computation.4 | async-start | bytes 9437184 | tf_op jit(solution)/shard_map/reduce_scatter | solution.py:52
  330.5 6.5 copy-start.2
  348.9 127.1 %copy-start.3 = (s32[1,16]{1,0:T(1,128)S(1)}, s32[1,16]{1,0:T(1,128)}, u32[]{:S(2)}) copy-start(s32[1,16]{1,0:T(1,128)} %param.8) | copy-start | bytes 196
  479.6 145.6 %slice-start = ((s8[6291456]{0:T(1024)(128)(4,1)}), s8[4194304]{0:T(1024)(128)(4,1)S(1)}, s32[]{:S(2)}) async-start(s8[6291456]{0:T(1024)(128)(4,1)} %bitcast.49), calls=%async_computation.5 | async-start | bytes 8388608
  483.3 142.0 %slice-start.1 = ((s8[6291456]{0:T(1024)(128)(4,1)}), s8[2097152]{0:T(1024)(128)(4,1)S(1)}, s32[]{:S(2)}) async-start(s8[6291456]{0:T(1024)(128)(4,1)} %bitcast.49), calls=%async_computation.6 | async-start | bytes 4194304
  483.3 157.9 %copy-start.1 = (bf16[512,2048]{1,0:T(8,128)(2,1)S(1)}, bf16[512,2048]{1,0:T(8,128)(2,1)}, u32[]{:S(2)}) copy-start(bf16[512,2048]{1,0:T(8,128)(2,1)} %param.5) | copy-start | bytes 6291460
Sparse Core Ops, SparseCore 0:
  629.1 12.1 reduce-scatter.1
